TPU v7x, 512 devices: a whole 4x8x8 slice. The times are simulated.
512 devices in a mesh: outer: 16 (over z, core), inner: 32 (over x, y).
Axes of the slice: x: 4, y: 8, z: 8, core: 2. Of those that a mesh axis runs over, the one named last changes fastest.
Arguments:
- queries: bfloat16 [65536, 2048], P(('outer', 'inner')), may hold values from -6 to 6
- keys: bfloat16 [65536, 2048], P(('outer', 'inner')), may hold values from -6 to 6
- values: bfloat16 [65536, 2048], P(('outer', 'inner')), may hold values from -6 to 6
- cotangent: bfloat16 [65536, 2048], P(('outer', 'inner')), may hold values from -6 to 6
Outputs:
- attended: bfloat16 [65536, 2048], P(('outer', 'inner'))
- grad_queries: bfloat16 [65536, 2048], P(('outer', 'inner'))
- grad_keys: bfloat16 [65536, 2048], P(('outer', 'inner'))
- grad_values: bfloat16 [65536, 2048], P(('outer', 'inner'))
All inputs are finite; a program needn't handle non-finite values.
Results may differ from a plain program's by a relative error of at most 0.013.
Values may be sent and summed in bfloat16 or wider, within the bound.
A program may use at most 64 MiB of HBM per device.

v0:
```python
import jax
import jax.numpy as jnp
from jax import lax
from jax.sharding import PartitionSpec as P

HEADS = 16
HEAD = 128
BLOCK = 512


def carried_in(x, axis, combine, identity, reverse):
    count, place = (lax.axis_size(axis), lax.axis_index(axis))
    everything = lax.all_gather(x, axis)
    start = jnp.broadcast_to(jnp.asarray(identity, x.dtype), x.shape)

    def turn(k, before):
        at = count - 1 - k if reverse else k
        reached = at > place if reverse else at < place
        new = combine(before, everything[at])
        return jnp.where(reached, new, before)

    return lax.fori_loop(0, count, turn, start)


def add_states(earlier, later):
    return earlier + later


def body(queries, keys, values, cotangent):
    rows = queries.shape[0]
    inner_count = lax.axis_size("inner")
    outer_count = lax.axis_size("outer")
    units = 2 * HEADS
    half = HEAD // 2
    width = HEADS * HEAD
    scale = float(HEAD * rows * inner_count * outer_count) ** (-0.5)
    lower = jnp.arange(BLOCK)[:, None] >= jnp.arange(BLOCK)[None, :]
    local_units = units // inner_count

    def doubled(x):
        return jnp.broadcast_to(x.reshape(rows, HEADS, 1, HEAD), (rows, HEADS, 2, HEAD)).reshape(
            rows, units, HEAD
        )

    packed = jnp.concatenate(
        [
            doubled(queries),
            doubled(keys),
            values.reshape(rows, units, half),
            cotangent.reshape(rows, units, half),
        ],
        axis=2,
    )
    arrived = lax.all_to_all(packed, "inner", split_axis=1, concat_axis=0, tiled=True)
    group = arrived.shape[0]
    nblocks = group // BLOCK
    blocks = arrived.reshape(nblocks, BLOCK, local_units, 3 * HEAD)
    q_all = blocks[..., :HEAD]
    k_all = blocks[..., HEAD : 2 * HEAD]
    v_all = blocks[..., 2 * HEAD : 2 * HEAD + half]
    d_all = blocks[..., 2 * HEAD + half :]
    kv_blocks = jnp.einsum("nsuk,nsuv->nukv", k_all, v_all, preferred_element_type=jnp.float32)
    qd_blocks = jnp.einsum("ntuk,ntuv->nukv", q_all, d_all, preferred_element_type=jnp.float32)
    own_qd = jnp.sum(qd_blocks, 0)
    kv_total = jnp.sum(kv_blocks, 0)
    before_kv = jnp.zeros_like(kv_total)
    after_qd = jnp.zeros_like(own_qd)
    state_shape = kv_total.shape
    zeros = jnp.zeros(state_shape, jnp.float32)
    carried_kv = carried_in(kv_total, "outer", add_states, zeros, False)
    carried_qd = carried_in(own_qd, "outer", add_states, zeros, True)
    s_before = (carried_kv + before_kv)[None] + jnp.cumsum(kv_blocks, 0) - kv_blocks
    g_after = (carried_qd + after_qd + own_qd)[None] - jnp.cumsum(qd_blocks, 0)

    def one_block(parts):
        qq, kk, vv, dd, state, adjoint = parts
        s_round = state.astype(jnp.bfloat16)
        g_round = adjoint.astype(jnp.bfloat16)
        scores = jnp.einsum("tuk,suk->uts", qq, kk, preferred_element_type=jnp.float32)
        a_round = jnp.where(lower[None], scores, 0.0).astype(jnp.bfloat16)
        back = jnp.einsum("tuv,suv->uts", dd, vv, preferred_element_type=jnp.float32)
        b_round = jnp.where(lower[None], back, 0.0).astype(jnp.bfloat16)
        attended = scale * (
            jnp.einsum("tuk,ukv->tuv", qq, s_round, preferred_element_type=jnp.float32)
            + jnp.einsum("uts,suv->tuv", a_round, vv, preferred_element_type=jnp.float32)
        )
        part_q = scale * (
            jnp.einsum("tuv,ukv->tuk", dd, s_round, preferred_element_type=jnp.float32)
            + jnp.einsum("uts,suk->tuk", b_round, kk, preferred_element_type=jnp.float32)
        )
        part_k = scale * (
            jnp.einsum("suv,ukv->suk", vv, g_round, preferred_element_type=jnp.float32)
            + jnp.einsum("uts,tuk->suk", b_round, qq, preferred_element_type=jnp.float32)
        )
        grad_v = scale * (
            jnp.einsum("suk,ukv->suv", kk, g_round, preferred_element_type=jnp.float32)
            + jnp.einsum("uts,tuv->suv", a_round, dd, preferred_element_type=jnp.float32)
        )
        return (attended.astype(jnp.bfloat16), grad_v.astype(jnp.bfloat16), part_q, part_k)

    attended, grad_v, part_q, part_k = lax.map(
        one_block, (q_all, k_all, v_all, d_all, s_before, g_after)
    )
    attended = attended.reshape(group, local_units, half)
    grad_v = grad_v.reshape(group, local_units, half)
    part_q = part_q.reshape(group, local_units, HEAD)
    part_k = part_k.reshape(group, local_units, HEAD)
    light = jnp.concatenate([attended, grad_v], axis=2)
    heavy = jnp.concatenate([part_q, part_k], axis=2)
    light_back, heavy_back = (
        lax.all_to_all(
            light.astype(jnp.float32), "inner", split_axis=0, concat_axis=1, tiled=True
        ).astype(light.dtype),
        lax.all_to_all(heavy, "inner", split_axis=0, concat_axis=1, tiled=True),
    )
    light_four = light_back.reshape(rows, HEADS, 2, HEAD)
    heavy_four = heavy_back.reshape(rows, HEADS, 2, 2 * HEAD)
    summed = heavy_four[:, :, 0] + heavy_four[:, :, 1]
    out_main = light_four[..., :half].reshape(rows, width)
    out_values = light_four[..., half:].reshape(rows, width)
    out_queries = summed[..., :HEAD].reshape(rows, width).astype(jnp.bfloat16)
    out_keys = summed[..., HEAD:].reshape(rows, width).astype(jnp.bfloat16)
    return (out_main, out_queries, out_keys, out_values)


def solution(mesh):
    in_specs = (
        P(("outer", "inner"), None),
        P(("outer", "inner"), None),
        P(("outer", "inner"), None),
        P(("outer", "inner"), None),
    )
    out_specs = (
        P(("outer", "inner"), None),
        P(("outer", "inner"), None),
        P(("outer", "inner"), None),
        P(("outer", "inner"), None),
    )
    return jax.shard_map(body, mesh=mesh, in_specs=in_specs, out_specs=out_specs, check_vma=False)
```

profile of v0, /device:TPU:6, one launch (start us, length us, event | category | flops | bytes accessed | tf_op | source)
XLA Modules:
  0.0 442.5 jit_solution(10289348364403049257)
XLA Ops:
  2.6 1.2 copy_bitcast_fusion
  3.8 1.3 copy.77
  6.6 1.5 copy.80
  8.1 1.3 broadcast_in_dim.44
  9.6 2.6 pad_maximum_fusion.1
  12.3 10.4 %all-to-all-start = ((bf16[128,32,384]{2,0,1:T(8,128)(2,1)}), bf16[128,32,384]{2,0,1:T(8,128)(2,1)}, u32[]{:S(2)}, u32[]{:S(2)}) async-start(bf16[128,32,384]{2,0,1:T(8,128)(2,1)} %pad_maximum_fusion.1), calls=%async_computation | async-start | bytes 6291456 | tf_op jit(solution)/shard_map/all_to_all | solution.py:54
  22.8 72.6 %all-to-all-done = bf16[128,32,384]{2,0,1:T(8,128)(2,1)} async-done(((bf16[128,32,384]{2,0,1:T(8,128)(2,1)}), bf16[128,32,384]{2,0,1:T(8,128)(2,1)}, u32[]{:S(2)}, u32[]{:S(2)}) %all-to-all-start) | async-done | bytes 3145760 | tf_op jit(solution)/shard_map/all_to_all | solution.py:54
  95.4 3.3 fusion.82
  98.6 2.8 fusion.81
  101.4 2.7 slice_bitcast_fusion.1
  104.1 3.1 fusion.78
  107.2 24.5 %all-gather = f32[2048,64]{0,1:T(8,128)S(1)} all-gather(f32[128,64]{0,1:T(8,128)S(1)} %get-tuple-element.473), channel_id=2, replica_groups=mesh['outer'=16,'inner'=32] {'outer'}, dimensions={0}, use_global_device_ids=true | all-gather | bytes 557056 | tf_op jit(solution)/shard_map/all_gather | solution.py:13
  131.7 1.3 copy.108
  133.0 14.1 %while.49 = (s32[]{:T(128)}, f32[1,128,64]{2,1,0:T(8,128)S(1)}, s32[]{:T(128)}, f32[16,1,128,64]{3,2,1,0:T(8,128)}, s32[]{:T(128)}, /*index=5*/s32[]{:T(128)}) while((s32[]{:T(128)}, f32[1,128,64]{2,1,0:T(8,128)S(1)}, s32[]{:T(128)}, f32[16,1,128,64]{3,2,1,0:T(8,128)}, s32[]{:T(128)}, /*index=5*/s32[]{:T(128)}) %tuple.123), condition=%wide.region_2.3_spmd.clone, body=%wide.region_1.0_spmd.clone.sunk | while | flops 24580 | bytes 98405 | solution.py:22
  147.2 15.9 %all-gather.1 = f32[2048,64]{0,1:T(8,128)S(1)} all-gather(f32[128,64]{0,1:T(8,128)S(1)} %get-tuple-element.475), channel_id=3, replica_groups=mesh['outer'=16,'inner'=32] {'outer'}, dimensions={0}, use_global_device_ids=true | all-gather | bytes 557056 | tf_op jit(solution)/shard_map/all_gather | solution.py:13
  163.1 1.3 copy.109
  164.4 14.2 %while.50 = (s32[]{:T(128)}, f32[1,128,64]{2,1,0:T(8,128)S(1)}, s32[]{:T(128)}, f32[16,1,128,64]{3,2,1,0:T(8,128)}, s32[]{:T(128)}, /*index=5*/s32[]{:T(128)}, s32[]{:T(128)}, s32[]{:T(128)}) while((s32[]{:T(128)}, f32[1,128,64]{2,1,0:T(8,128)S(1)}, s32[]{:T(128)}, f32[16,1,128,64]{3,2,1,0:T(8,128)}, s32[]{:T(128)}, ...), condition=%wide.region_6.7_spmd.clone, body=%wide.region_5.6_spmd.clone.sunk | while | flops 24584 | bytes 98467 | solution.py:22
  178.7 1.5 copy.118
  181.4 1.7 fusion.64
  184.1 88.3 %while.48 = (s32[]{:T(128)}, bf16[8,512,1,64]{1,3,2,0:T(8,128)(2,1)}, bf16[8,512,1,64]{1,3,2,0:T(8,128)(2,1)}, f32[8,512,1,128]{3,1,0,2:T(8,128)}, f32[8,512,1,1...) while((s32[]{:T(128)}, ...), condition=%wide.region_9.10_spmd.clone.clone, body=%wide.region_8.9_spmd.clone.clone.sunk | while | flops 337575936 | bytes 8884385 | solution.py:101
  187.5 1.2 fusion.146
  190.5 1.2 fusion.141
  192.5 1.8 fusion.142
  201.5 1.2 fusion.141
  203.6 1.8 fusion.142
  212.6 1.2 fusion.141
  214.6 1.8 fusion.142
  220.7 1.2 fusion.146
  223.6 1.2 fusion.141
  225.7 1.8 fusion.142
  234.6 1.2 fusion.141
  236.7 1.8 fusion.142
  242.7 1.2 fusion.146
  245.6 1.2 fusion.141
  247.7 1.8 fusion.142
  253.7 1.2 fusion.146
  256.7 1.2 fusion.141
  258.7 1.8 fusion.142
  267.7 1.2 fusion.141
  269.7 1.8 fusion.142
  274.7 3.7 copy.95
  278.5 7.8 %all-to-all-start.1 = ((f32[4096,1,128]{2,1,0:T(1,128)}), f32[4096,1,128]{2,1,0:T(1,128)S(1)}, u32[]{:S(2)}, u32[]{:S(2)}) async-start(f32[4096,1,128]{2,1,0:T(1,128)} %copy.95), calls=%async_computation.1 | async-start | bytes 4194304 | tf_op jit(solution)/shard_map/all_to_all | solution.py:111
  286.2 2.5 pad_maximum_fusion
  288.7 19.2 %copy.100 = f32[4096,1,256]{2,1,0:T(1,128)} copy(f32[4096,1,256]{2,0,1:T(8,128)S(1)} %pad_maximum_fusion) | data formatting | bytes 8388608 | tf_op jit(solution)/shard_map/concatenate | solution.py:109
  307.9 26.8 %all-to-all-done.1 = f32[4096,1,128]{2,1,0:T(1,128)S(1)} async-done(((f32[4096,1,128]{2,1,0:T(1,128)}), f32[4096,1,128]{2,1,0:T(1,128)S(1)}, u32[]{:S(2)}, u32[]{:S(2)}) %all-to-all-start.1) | async-done | bytes 2097184 | tf_op jit(solution)/shard_map/all_to_all | solution.py:111
  334.7 8.6 %all-to-all-start.2 = ((f32[4096,1,256]{2,1,0:T(1,128)}), f32[4096,1,256]{2,1,0:T(1,128)}, u32[]{:S(2)}, u32[]{:S(2)}) async-start(f32[4096,1,256]{2,1,0:T(1,128)} %copy.100), calls=%async_computation.2 | async-start | bytes 8388608 | tf_op jit(solution)/shard_map/all_to_all | solution.py:114
  346.7 90.2 %all-to-all-done.2 = f32[4096,1,256]{2,1,0:T(1,128)} async-done(((f32[4096,1,256]{2,1,0:T(1,128)}), f32[4096,1,256]{2,1,0:T(1,128)}, u32[]{:S(2)}, u32[]{:S(2)}) %all-to-all-start.2) | async-done | bytes 4194336 | tf_op jit(solution)/shard_map/all_to_all | solution.py:114
  436.9 2.5 copy.116
  (182 shorter events, 101.5 us)
Async XLA Ops:
  0.6 1.0 copy-start
  1.7 3.9 copy-start.1
  12.3 83.1 %all-to-all-start = ((bf16[128,32,384]{2,0,1:T(8,128)(2,1)}), bf16[128,32,384]{2,0,1:T(8,128)(2,1)}, u32[]{:S(2)}, u32[]{:S(2)}) async-start(bf16[128,32,384]{2,0,1:T(8,128)(2,1)} %pad_maximum_fusion.1), calls=%async_computation | async-start | bytes 6291456 | tf_op jit(solution)/shard_map/all_to_all | solution.py:54
  278.5 56.3 %all-to-all-start.1 = ((f32[4096,1,128]{2,1,0:T(1,128)}), f32[4096,1,128]{2,1,0:T(1,128)S(1)}, u32[]{:S(2)}, u32[]{:S(2)}) async-start(f32[4096,1,128]{2,1,0:T(1,128)} %copy.95), calls=%async_computation.1 | async-start | bytes 4194304 | tf_op jit(solution)/shard_map/all_to_all | solution.py:111
  334.7 102.2 %all-to-all-start.2 = ((f32[4096,1,256]{2,1,0:T(1,128)}), f32[4096,1,256]{2,1,0:T(1,128)}, u32[]{:S(2)}, u32[]{:S(2)}) async-start(f32[4096,1,256]{2,1,0:T(1,128)} %copy.100), calls=%async_computation.2 | async-start | bytes 8388608 | tf_op jit(solution)/shard_map/all_to_all | solution.py:114
where the time goes:
time: 450 us; the launch traced here: 443 us
  waiting for transfers between devices  190 us (42%)
  matrix products  77.1 us (17%)
  local copies, waits for them, and re-layouts  70.3 us (16%)
  blocking collectives  40.4 us (9%)
  other arithmetic  35.9 us (8%)
  starting transfers between devices  26.8 us (6%)
    all_to_all x1, waiting for transfers between devices, body(): lax.all_to_all(heavy, 'inner', split_axis=0, concat_axis=1, tiled=True)  90.2 us
    all_to_all x1, waiting for transfers between devices, body(): lax.all_to_all(packed, 'inner', split_axis=1, concat_axis=0, tiled=True)  72.6 us
    all_gather x2, blocking collectives, carried_in(): everything = lax.all_gather(x, axis)  40.4 us
    select_n x32, other arithmetic, turn(): return jnp.where(reached, new, before)  27.5 us
    all_to_all x1, waiting for transfers between devices, body(): lax.all_to_all(light.astype(jnp.float32), 'inner', split_axis=0, concat_a...  26.8 us
    concatenate x1, local copies, waits for them, and re-layouts, body(): heavy = jnp.concatenate([part_q, part_k], axis=2)  19.2 us
    unnamed x18, local copies, waits for them, and re-layouts  18.7 us
    dot_general x8, matrix products, one_block(): jnp.einsum('uts,suv->tuv', a_round, vv, preferred_element_type=jnp.float32)  14.1 us
  transfers between devices with their start and end apart: 3, of which 3 were waited for; matrix products, arithmetic and copies ran while one was open for 6% of the time, Pallas kernels for 0%

commit v1 on v0

v1 whole, which is shorter than its diff:
```python
import functools

import jax
import jax.numpy as jnp
from jax import lax
from jax.experimental import pallas as pl
from jax.experimental.pallas import tpu as pltpu
from jax.sharding import PartitionSpec as P

HEAD = 128


def dot(a, b, over_a, over_b):
    return lax.dot_general(
        a, b, (((over_a,), (over_b,)), ((), ())), preferred_element_type=jnp.float32
    )


def states_kernel(heads, q_ref, k_ref, v_ref, d_ref, out_ref):
    for h in range(heads):
        cols = slice(h * HEAD, (h + 1) * HEAD)
        out_ref[h] = dot(k_ref[:, cols], v_ref[:, cols], 0, 0).astype(out_ref.dtype)
        out_ref[heads + h] = dot(q_ref[:, cols], d_ref[:, cols], 0, 0).astype(out_ref.dtype)


def outputs_kernel(heads, scale, q_ref, k_ref, v_ref, d_ref, s_ref, o_ref, gq_ref, gk_ref, gv_ref):
    rows = q_ref.shape[0]
    lower = lax.broadcasted_iota(jnp.int32, (rows, rows), 0) >= lax.broadcasted_iota(
        jnp.int32, (rows, rows), 1
    )
    for h in range(heads):
        cols = slice(h * HEAD, (h + 1) * HEAD)
        q, k, v, d = q_ref[:, cols], k_ref[:, cols], v_ref[:, cols], d_ref[:, cols]
        s, g = s_ref[h], s_ref[heads + h]
        a = jnp.where(lower, dot(q, k, 1, 1), 0.0).astype(jnp.bfloat16)
        b = jnp.where(lower, dot(d, v, 1, 1), 0.0).astype(jnp.bfloat16)
        o_ref[:, cols] = (scale * (dot(q, s, 1, 0) + dot(a, v, 1, 0))).astype(o_ref.dtype)
        gq_ref[:, cols] = (scale * (dot(d, s, 1, 1) + dot(b, k, 1, 0))).astype(gq_ref.dtype)
        gk_ref[:, cols] = (scale * (dot(v, g, 1, 1) + dot(b, q, 0, 0))).astype(gk_ref.dtype)
        gv_ref[:, cols] = (scale * (dot(k, g, 1, 0) + dot(a, d, 0, 0))).astype(gv_ref.dtype)


def body(queries, keys, values, cotangent):
    rows, width = queries.shape
    heads = width // HEAD
    inner, outer = lax.axis_size("inner"), lax.axis_size("outer")
    scale = float(HEAD * rows * inner * outer) ** (-0.5)
    slabs = 2 * heads
    own = slabs // inner
    vmem = pl.BlockSpec(memory_space=pltpu.VMEM)

    states = pl.pallas_call(
        functools.partial(states_kernel, heads),
        out_shape=jax.ShapeDtypeStruct((slabs, HEAD, HEAD), jnp.bfloat16),
        in_specs=[vmem] * 4,
        out_specs=vmem,
    )(queries, keys, values, cotangent)

    arrived = lax.all_to_all(states, "inner", split_axis=0, concat_axis=0, tiled=True)
    arrived = arrived.reshape(inner, own, HEAD, HEAD)
    slab = lax.axis_index("inner") * own
    before = slab < heads
    at = jnp.arange(inner)
    reach = jnp.where(before, at[None, :] < at[:, None], at[None, :] > at[:, None])
    within = jnp.einsum(
        "ij,jukv->iukv", reach.astype(jnp.bfloat16), arrived, preferred_element_type=jnp.float32
    )
    total = jnp.sum(arrived.astype(jnp.float32), 0)
    everything = lax.all_gather(total, "outer")
    place, group = lax.axis_index("outer"), jnp.arange(outer)
    reached = jnp.where(before, group < place, group > place)
    carried = jnp.sum(jnp.where(reached[:, None, None, None], everything, 0.0), 0)
    whole = (within + carried[None]).astype(jnp.bfloat16).reshape(slabs, HEAD, HEAD)
    state = lax.all_to_all(whole, "inner", split_axis=0, concat_axis=0, tiled=True)

    return pl.pallas_call(
        functools.partial(outputs_kernel, heads, scale),
        out_shape=(jax.ShapeDtypeStruct((rows, width), jnp.bfloat16),) * 4,
        in_specs=[vmem] * 5,
        out_specs=(vmem,) * 4,
    )(queries, keys, values, cotangent, state)


def solution(mesh):
    spec = P(("outer", "inner"), None)
    return jax.shard_map(
        body, mesh=mesh, in_specs=(spec,) * 4, out_specs=(spec,) * 4, check_vma=False
    )
```

time: 450 us -> 147 us (0.33); the launches traced: 443 us -> 145 us
  waiting for transfers between devices: 190 us -> 43 us
  matrix products: 77.1 us -> 0.72 us
  local copies, waits for them, and re-layouts: 70.3 us -> 0 us
  blocking collectives: 40.4 us -> 73.2 us
  other arithmetic: 35.9 us -> 3.38 us
  starting transfers between devices: 26.8 us -> 0.04 us
  between operations: 0.9 us -> 14.1 us
  Pallas kernels: 0 us -> 10.2 us
    all_to_all x3 -> x0, waiting for transfers between devices: 190 us -> none  [the longest x1 90.2 us: body(): lax.all_to_all(heavy, 'inner', split_axis=0, concat_axis=1, tiled=True)]
    dot_general x82 -> x1, matrix products: 77.1 us -> 0.72 us  [body(): jnp.einsum('ij,jukv->iukv', reach.astype(jnp.bfloat16), arrived, preferre...]
    all_to_all x0 -> x2, blocking collectives: none -> 73.2 us  [the longest x1 36.6 us: body(): lax.all_to_all(states, 'inner', split_axis=0, concat_axis=0, tiled=True)]
    all_gather x0 -> x1, waiting for transfers between devices: none -> 43 us  [body(): everything = lax.all_gather(total, 'outer')]
    all_gather x2 -> x0, blocking collectives: 40.4 us -> none  [carried_in(): everything = lax.all_gather(x, axis)]
    select_n x32 -> x1, other arithmetic: 27.5 us -> 0.01 us  [body(): reached = jnp.where(before, group < place, group > place)]
    all_to_all x3 -> x0, starting transfers between devices: 26.8 us -> none  [the longest x1 10.4 us: body(): lax.all_to_all(packed, 'inner', split_axis=1, concat_axis=0, tiled=True)]
    concatenate x3 -> x0, local copies, waits for them, and re-layouts: 21.3 us -> none  [the longest x1 19.2 us: body(): heavy = jnp.concatenate([part_q, part_k], axis=2)]
  transfers between devices with their start and end apart: 3 -> 1, of which waited for: 3 -> 1; matrix products, arithmetic and copies ran while one was open for 6% -> 1% of each run, Pallas kernels for 0% -> 0%
where the time goes in v1:
time: 147 us; the launch traced here: 145 us
  blocking collectives  73.2 us (50%)
  waiting for transfers between devices  43 us (29%)
  between operations  14.1 us (10%)
  Pallas kernels  10.2 us (7%)
  other arithmetic  3.38 us (2%)
    all_gather x1, waiting for transfers between devices, body(): everything = lax.all_gather(total, 'outer')  43 us
    all_to_all x1, blocking collectives, body(): lax.all_to_all(states, 'inner', split_axis=0, concat_axis=0, tiled=True)  36.6 us
    all_to_all x1, blocking collectives, body(): lax.all_to_all(whole, 'inner', split_axis=0, concat_axis=0, tiled=True)  36.6 us
    pallas_call x1, Pallas kernels, body(): pl.pallas_call(functools.partial(outputs_kernel, heads, scale), out_shape...  7.2 us
    pallas_call x1, Pallas kernels, body(): pl.pallas_call(functools.partial(states_kernel, heads), out_shape=jax.Sha...  2.98 us
  transfers between devices with their start and end apart: 1, of which 1 were waited for; matrix products, arithmetic and copies ran while one was open for 1% of the time, Pallas kernels for 0%

profile of v1, /device:TPU:6, one launch (start us, length us, event | category | flops | bytes accessed | tf_op | source)
XLA Modules:
  0.0 144.6 jit_solution(4230799941837393204)
XLA Ops:
  7.2 0.0 all-gather.3.cloned.1.call-start
  7.2 3.0 %shard_map.75 = bf16[32,128,128]{2,1,0:T(8,128)(2,1)} custom-call(bf16[128,2048]{1,0:T(8,128)(2,1)} %q_ref.3, bf16[128,2048]{1,0:T(8,128)(2,1)} %k_ref.3, bf16[128,2048]{1,0:T(8,128)(2,1)} %v_ref.3, bf16[128,2048]{1,0:T(8,128)(2,1)} %d_ref.3), custom_call_target="tpu_custom_call" | custom-call | tf_op jit(solution)/shard_map/pallas_call | solution.py:52
  10.2 36.6 %all_to_all.10 = bf16[32,128,128]{2,1,0:T(8,128)(2,1)S(1)} all-to-all(bf16[32,128,128]{2,1,0:T(8,128)(2,1)} %shard_map.75), channel_id=1, replica_groups=mesh['outer'=16,'inner'=32] {'inner'}, dimensions={0} | all-to-all | bytes 2097152 | tf_op jit(solution)/shard_map/all_to_all | solution.py:59
  46.8 0.8 convert_reduce_fusion
  47.6 0.0 all-gather.3.cloned.1.call-update
  47.7 0.7 fusion.1
  48.4 43.0 %all-gather.3.cloned.1.call-done = f32[2048,128]{1,0:T(8,128)} async-done(((f32[128,128]{1,0:T(8,128)}), f32[2048,128]{1,0:T(8,128)}) %all-gather.3.cloned.1.call-update) | async-done | bytes 1048592 | tf_op jit(solution)/shard_map/all_gather | solution.py:69
  91.4 1.4 select_reduce_fusion
  92.8 1.2 fusion
  94.0 36.6 %all_to_all.11.s_ref = bf16[32,128,128]{2,1,0:T(8,128)(2,1)} all-to-all(bf16[32,128,128]{2,1,0:T(8,128)(2,1)S(1)} %fusion), channel_id=1, replica_groups=mesh['outer'=16,'inner'=32] {'inner'}, dimensions={0} | all-to-all | bytes 2097152 | tf_op jit(solution)/shard_map/all_to_all | solution.py:74
  130.6 7.2 %shard_map.76 = (bf16[128,2048]{1,0:T(8,128)(2,1)}, bf16[128,2048]{1,0:T(8,128)(2,1)}, bf16[128,2048]{1,0:T(8,128)(2,1)}, bf16[128,2048]{1,0:T(8,128)(2,1)}) custom-call(bf16[128,2048]{1,0:T(8,128)(2,1)} %q_ref.3, bf16[128,2048]{1,0:T(8,128)(2,1)} %k_ref.3, bf16[128,2048]{1,0:T(8,128)(2,1)} %v_ref.3, bf16[128,2048]{1,0:T(8,128)(2,1)} %d_ref.3, ...), custom_call_target="tpu_custom_call" | custom-call | tf_op jit(solution)/shard_map/pallas_call | solution.py:76
  (1 shorter events, 0.0 us)
Async XLA Ops:
  7.2 84.2 %all-gather.3.cloned.1.call-start = ((), (), s32[]{:S(2)}) async-start(), calls=%async_computation.2 | async-start | bytes 1114112 | tf_op jit(solution)/shard_map/all_gather | solution.py:69
Sparse Core Ops, SparseCore 0:
  47.8 43.6 all-gather.2

commit v2 on v1

--- a/solution.py
+++ b/solution.py
@@ -8,6 +8,7 @@
 from jax.sharding import PartitionSpec as P
 
 HEAD = 128
+MESH = pl.DeviceIdType.MESH
 
 
 def dot(a, b, over_a, over_b):
@@ -16,11 +17,137 @@
     )
 
 
-def states_kernel(heads, q_ref, k_ref, v_ref, d_ref, out_ref):
+def exchange_kernel(
+    heads, inner, outer, q_ref, k_ref, v_ref, d_ref, state_ref,
+    states, arrived, prefix, outgoing, total, mate, pair, pairs, carried,
+    in_send, in_recv, z_send, z_recv, out_send, out_recv, core_send, core_recv,
+):
+    me, place = lax.axis_index("inner"), lax.axis_index("outer")
+    chips, half = outer // 2, HEAD // 2
+    z, core = place // 2, place % 2
+    other = (place + 1 - 2 * core, me)
+    later = me // heads
+    my_rows = pl.ds(pl.multiple_of(core * half, half), half)
+    other_rows = pl.ds(pl.multiple_of((1 - core) * half, half), half)
+
+    def in_copy(peer, source):
+        return pltpu.make_async_remote_copy(
+            states.at[peer], arrived.at[source], in_send.at[peer], in_recv.at[source],
+            device_id=(place, peer), device_id_type=MESH,
+        )
+
+    def z_copy(peer, source):
+        return pltpu.make_async_remote_copy(
+            pair, pairs.at[source], z_send.at[peer], z_recv.at[source],
+            device_id=(peer * 2 + core, me), device_id_type=MESH,
+        )
+
+    def out_copy(peer, source):
+        return pltpu.make_async_remote_copy(
+            outgoing.at[peer], state_ref.at[source], out_send.at[peer], out_recv.at[source],
+            device_id=(place, peer), device_id_type=MESH,
+        )
+
+    def total_copy():
+        return pltpu.make_async_remote_copy(
+            total, mate, core_send.at[0], core_recv.at[0], device_id=other, device_id_type=MESH
+        )
+
+    def carried_copy(rows):
+        return pltpu.make_async_remote_copy(
+            carried.at[rows], carried.at[rows], core_send.at[1], core_recv.at[1],
+            device_id=other, device_id_type=MESH,
+        )
+
+    barrier = pltpu.get_barrier_semaphore()
+
+    @pl.loop(1, inner)
+    def _(step):
+        pl.semaphore_signal(
+            barrier, inc=1, device_id=(place, (me + step) % inner), device_id_type=MESH
+        )
+
+    @pl.loop(1, chips)
+    def _(step):
+        pl.semaphore_signal(
+            barrier, inc=1, device_id=((z + step) % chips * 2 + core, me), device_id_type=MESH
+        )
+
+    pl.semaphore_signal(barrier, inc=1, device_id=other, device_id_type=MESH)
+
     for h in range(heads):
         cols = slice(h * HEAD, (h + 1) * HEAD)
-        out_ref[h] = dot(k_ref[:, cols], v_ref[:, cols], 0, 0).astype(out_ref.dtype)
-        out_ref[heads + h] = dot(q_ref[:, cols], d_ref[:, cols], 0, 0).astype(out_ref.dtype)
+        states[h] = dot(k_ref[:, cols], v_ref[:, cols], 0, 0).astype(states.dtype)
+        states[heads + h] = dot(q_ref[:, cols], d_ref[:, cols], 0, 0).astype(states.dtype)
+
+    pl.semaphore_wait(barrier, inner - 1 + chips - 1 + 1)
+
+    @pl.loop(1, inner)
+    def _(step):
+        in_copy((me + step) % inner, me).start()
+
+    own = states[me]
+    arrived[me] = own
+
+    def add_arrived(step, acc):
+        source = (me + inner - step) % inner
+        in_copy(source, source).wait_recv()
+        return acc + arrived[source].astype(jnp.float32)
+
+    total[...] = lax.fori_loop(1, inner, add_arrived, own.astype(jnp.float32))
+    total_copy().start()
+
+    def turn(step, acc):
+        at = step + later * (inner - 1 - 2 * step)
+        prefix[at] = acc
+        return acc + arrived[at].astype(jnp.float32)
+
+    lax.fori_loop(0, inner, turn, jnp.zeros((HEAD, HEAD), jnp.float32))
+
+    total_copy().wait_recv()
+    pair[...] = (total[my_rows] + mate[my_rows]).astype(pair.dtype)
+
+    @pl.loop(1, chips)
+    def _(step):
+        z_copy((z + step) % chips, z).start()
+
+    def add_pair(step, acc):
+        source = (z + chips - step) % chips
+        z_copy(source, source).wait_recv()
+        reached = (source - z) * (2 * later - 1) > 0
+        return acc + jnp.where(reached, pairs[source].astype(jnp.float32), 0.0)
+
+    carried[my_rows] = lax.fori_loop(1, chips, add_pair, jnp.zeros((half, HEAD), jnp.float32))
+    carried_copy(my_rows).start()
+    carried_copy(other_rows).wait_recv()
+    offset = carried[...] + jnp.where(core + later == 1, mate[...], 0.0)
+
+    outgoing[me] = (prefix[me] + offset).astype(outgoing.dtype)
+    state_ref[me] = (prefix[me] + offset).astype(outgoing.dtype)
+
+    @pl.loop(1, inner)
+    def _(step):
+        peer = (me + step) % inner
+        outgoing[peer] = (prefix[peer] + offset).astype(outgoing.dtype)
+        out_copy(peer, me).start()
+
+    @pl.loop(1, inner)
+    def _(step):
+        source = (me + inner - step) % inner
+        out_copy(source, source).wait_recv()
+
+    @pl.loop(1, inner)
+    def _(step):
+        peer = (me + step) % inner
+        in_copy(peer, me).wait_send()
+        out_copy(peer, me).wait_send()
+
+    @pl.loop(1, chips)
+    def _(step):
+        z_copy((z + step) % chips, z).wait_send()
+
+    total_copy().wait_send()
+    carried_copy(my_rows).wait_send()
 
 
 def outputs_kernel(heads, scale, q_ref, k_ref, v_ref, d_ref, s_ref, o_ref, gq_ref, gk_ref, gv_ref):
@@ -46,32 +173,31 @@
     inner, outer = lax.axis_size("inner"), lax.axis_size("outer")
     scale = float(HEAD * rows * inner * outer) ** (-0.5)
     slabs = 2 * heads
-    own = slabs // inner
+    assert slabs == inner
+    chips, half = outer // 2, HEAD // 2
     vmem = pl.BlockSpec(memory_space=pltpu.VMEM)
-
-    states = pl.pallas_call(
-        functools.partial(states_kernel, heads),
+    dma = pltpu.SemaphoreType.DMA
+
+    state = pl.pallas_call(
+        functools.partial(exchange_kernel, heads, inner, outer),
         out_shape=jax.ShapeDtypeStruct((slabs, HEAD, HEAD), jnp.bfloat16),
         in_specs=[vmem] * 4,
         out_specs=vmem,
+        scratch_shapes=[
+            pltpu.VMEM((slabs, HEAD, HEAD), jnp.bfloat16),
+            pltpu.VMEM((slabs, HEAD, HEAD), jnp.bfloat16),
+            pltpu.VMEM((slabs, HEAD, HEAD), jnp.float32),
+            pltpu.VMEM((slabs, HEAD, HEAD), jnp.bfloat16),
+            pltpu.VMEM((HEAD, HEAD), jnp.float32),
+            pltpu.VMEM((HEAD, HEAD), jnp.float32),
+            pltpu.VMEM((half, HEAD), jnp.bfloat16),
+            pltpu.VMEM((chips, half, HEAD), jnp.bfloat16),
+            pltpu.VMEM((HEAD, HEAD), jnp.float32),
+            dma((inner,)), dma((inner,)), dma((chips,)), dma((chips,)),
+            dma((inner,)), dma((inner,)), dma((2,)), dma((2,)),
+        ],
+        compiler_params=pltpu.CompilerParams(collective_id=0, has_side_effects=True),
     )(queries, keys, values, cotangent)
-
-    arrived = lax.all_to_all(states, "inner", split_axis=0, concat_axis=0, tiled=True)
-    arrived = arrived.reshape(inner, own, HEAD, HEAD)
-    slab = lax.axis_index("inner") * own
-    before = slab < heads
-    at = jnp.arange(inner)
-    reach = jnp.where(before, at[None, :] < at[:, None], at[None, :] > at[:, None])
-    within = jnp.einsum(
-        "ij,jukv->iukv", reach.astype(jnp.bfloat16), arrived, preferred_element_type=jnp.float32
-    )
-    total = jnp.sum(arrived.astype(jnp.float32), 0)
-    everything = lax.all_gather(total, "outer")
-    place, group = lax.axis_index("outer"), jnp.arange(outer)
-    reached = jnp.where(before, group < place, group > place)
-    carried = jnp.sum(jnp.where(reached[:, None, None, None], everything, 0.0), 0)
-    whole = (within + carried[None]).astype(jnp.bfloat16).reshape(slabs, HEAD, HEAD)
-    state = lax.all_to_all(whole, "inner", split_axis=0, concat_axis=0, tiled=True)
 
     return pl.pallas_call(
         functools.partial(outputs_kernel, heads, scale),

time: 147 us -> 87.1 us (0.59); the launches traced: 145 us -> 87 us
  Pallas kernels: 10.2 us -> 86.3 us
  blocking collectives: 73.2 us -> 0 us
  waiting for transfers between devices: 43 us -> 0 us
  between operations: 14.1 us -> 0.64 us
  other arithmetic: 3.38 us -> 0 us
    pallas_call x1, Pallas kernels: 2.98 us -> 79.1 us  [body(): pl.pallas_call(functools.partial(exchange_kernel, heads, inner, outer), o...]
    all_to_all x2 -> x0, blocking collectives: 73.2 us -> none  [the longest x1 36.6 us: body(): lax.all_to_all(states, 'inner', split_axis=0, concat_axis=0, tiled=True)]
    all_gather x1 -> x0, waiting for transfers between devices: 43 us -> none  [body(): everything = lax.all_gather(total, 'outer')]
    reduce_sum x2 -> x0, other arithmetic: 2.15 us -> none  [the longest x1 1.37 us: body(): jnp.sum(jnp.where(reached[:, None, None, None], everything, 0.0), 0)]
  transfers between devices with their start and end apart: 1 -> 0, of which waited for: 1 -> 0; matrix products, arithmetic and copies ran while one was open for 1% -> 0% of each run, Pallas kernels for 0% -> 0%
where the time goes in v2:
time: 87.1 us; the launch traced here: 87 us
  Pallas kernels  86.3 us (99%)
    pallas_call x1, Pallas kernels, body(): pl.pallas_call(functools.partial(exchange_kernel, heads, inner, outer), o...  79.1 us
    pallas_call x1, Pallas kernels, body(): pl.pallas_call(functools.partial(outputs_kernel, heads, scale), out_shape...  7.2 us

profile of v2, /device:TPU:6, one launch (start us, length us, event | category | flops | bytes accessed | tf_op | source)
XLA Modules:
  0.0 87.0 jit_solution(2734440323121305000)
XLA Ops:
  0.6 79.1 %shard_map.75.s_ref = bf16[32,128,128]{2,1,0:T(8,128)(2,1)} custom-call(bf16[128,2048]{1,0:T(8,128)(2,1)} %q_ref.3, bf16[128,2048]{1,0:T(8,128)(2,1)} %k_ref.3, bf16[128,2048]{1,0:T(8,128)(2,1)} %v_ref.3, bf16[128,2048]{1,0:T(8,128)(2,1)} %d_ref.3), custom_call_target="tpu_custom_call" | custom-call | tf_op jit(solution)/shard_map/pallas_call | solution.py:181
  79.8 7.2 %shard_map.76 = (bf16[128,2048]{1,0:T(8,128)(2,1)}, bf16[128,2048]{1,0:T(8,128)(2,1)}, bf16[128,2048]{1,0:T(8,128)(2,1)}, bf16[128,2048]{1,0:T(8,128)(2,1)}) custom-call(bf16[128,2048]{1,0:T(8,128)(2,1)} %q_ref.3, bf16[128,2048]{1,0:T(8,128)(2,1)} %k_ref.3, bf16[128,2048]{1,0:T(8,128)(2,1)} %v_ref.3, bf16[128,2048]{1,0:T(8,128)(2,1)} %d_ref.3, ...), custom_call_target="tpu_custom_call" | custom-call | tf_op jit(solution)/shard_map/pallas_call | solution.py:202

commit v3 on v1

v3 whole, which is shorter than its diff:
```python
import functools

import jax
import jax.numpy as jnp
from jax import lax
from jax.experimental import pallas as pl
from jax.experimental.pallas import tpu as pltpu
from jax.sharding import PartitionSpec as P

HEAD = 128
MESH = pl.DeviceIdType.MESH


def dot(a, b, over_a, over_b):
    return lax.dot_general(
        a, b, (((over_a,), (over_b,)), ((), ())), preferred_element_type=jnp.float32
    )


def exchange_kernel(
    heads, inner, outer, q_ref, k_ref, v_ref, d_ref, state_ref,
    states, arrived, prefix, outgoing, total, mate, pair, pairs, carried,
    in_send, in_recv, z_send, z_recv, out_send, out_recv, core_send, core_recv,
):
    me, place = lax.axis_index("inner"), lax.axis_index("outer")
    chips, half, quarter = outer // 2, HEAD // 2, HEAD // 4
    z, core = place // 2, place % 2
    other = (place + 1 - 2 * core, me)
    my_rows = pl.ds(pl.multiple_of(core * quarter, quarter), quarter)
    other_rows = pl.ds(pl.multiple_of((1 - core) * quarter, quarter), quarter)

    def in_copy(kind, peer, source):
        return pltpu.make_async_remote_copy(
            states.at[kind, peer], arrived.at[kind, source],
            in_send.at[kind, peer], in_recv.at[kind, source],
            device_id=(place, peer), device_id_type=MESH,
        )

    def z_copy(kind, peer, source):
        return pltpu.make_async_remote_copy(
            pair.at[kind], pairs.at[kind, source], z_send.at[kind, peer], z_recv.at[kind, source],
            device_id=(peer * 2 + core, me), device_id_type=MESH,
        )

    def state_at(kind, source):
        rows = pl.ds(pl.multiple_of(source // heads * half, half), half)
        return state_ref.at[kind, source % heads, rows]

    def out_copy(kind, peer, source):
        return pltpu.make_async_remote_copy(
            outgoing.at[kind, peer], state_at(kind, source),
            out_send.at[kind, peer], out_recv.at[kind, source],
            device_id=(place, peer), device_id_type=MESH,
        )

    def total_copy(kind):
        return pltpu.make_async_remote_copy(
            total.at[kind], mate.at[kind], core_send.at[0, kind], core_recv.at[0, kind],
            device_id=other, device_id_type=MESH,
        )

    def carried_copy(kind, rows):
        return pltpu.make_async_remote_copy(
            carried.at[kind, rows], carried.at[kind, rows],
            core_send.at[1, kind], core_recv.at[1, kind],
            device_id=other, device_id_type=MESH,
        )

    def make_states(kind, a_ref, b_ref):
        for h in range(heads):
            cols = slice(h * HEAD, (h + 1) * HEAD)
            both = dot(a_ref[:, cols], b_ref[:, cols], 0, 0).astype(states.dtype)
            states[kind, h] = both[:half]
            states[kind, heads + h] = both[half:]

    def send_states(kind):
        @pl.loop(1, inner)
        def _(step):
            in_copy(kind, (me + step) % inner, me).start()

        arrived[kind, me] = states[kind, me]

    def sum_within(kind):
        def add_arrived(step, acc):
            source = (me + inner - step) % inner
            in_copy(kind, source, source).wait_recv()
            return acc + arrived[kind, source].astype(jnp.float32)

        total[kind] = lax.fori_loop(1, inner, add_arrived, states[kind, me].astype(jnp.float32))
        total_copy(kind).start()

        def turn(step, acc):
            at = step if kind == 0 else inner - 1 - step
            prefix[kind, at] = acc
            return acc + arrived[kind, at].astype(jnp.float32)

        lax.fori_loop(0, inner, turn, jnp.zeros((half, HEAD), jnp.float32))

    def send_pair(kind):
        total_copy(kind).wait_recv()
        pair[kind] = (total[kind, my_rows] + mate[kind, my_rows]).astype(pair.dtype)

        @pl.loop(1, chips)
        def _(step):
            z_copy(kind, (z + step) % chips, z).start()

    def sum_across(kind):
        def add_pair(step, acc):
            source = (z + chips - step) % chips
            z_copy(kind, source, source).wait_recv()
            reached = source < z if kind == 0 else source > z
            return acc + jnp.where(reached, pairs[kind, source].astype(jnp.float32), 0.0)

        zeros = jnp.zeros((quarter, HEAD), jnp.float32)
        carried[kind, my_rows] = lax.fori_loop(1, chips, add_pair, zeros)
        carried_copy(kind, my_rows).start()
        carried_copy(kind, other_rows).wait_recv()

    def send_sums(kind):
        offset = carried[kind] + jnp.where(core + kind == 1, mate[kind], 0.0)

        @pl.loop(1, inner)
        def _(step):
            peer = (me + step) % inner
            outgoing[kind, peer] = (prefix[kind, peer] + offset).astype(outgoing.dtype)
            out_copy(kind, peer, me).start()

        state_at(kind, me)[...] = (prefix[kind, me] + offset).astype(outgoing.dtype)

    barrier = pltpu.get_barrier_semaphore()

    @pl.loop(1, inner)
    def _(step):
        pl.semaphore_signal(
            barrier, inc=1, device_id=(place, (me + step) % inner), device_id_type=MESH
        )

    @pl.loop(1, chips)
    def _(step):
        pl.semaphore_signal(
            barrier, inc=1, device_id=((z + step) % chips * 2 + core, me), device_id_type=MESH
        )

    pl.semaphore_signal(barrier, inc=1, device_id=other, device_id_type=MESH)
    make_states(0, k_ref, v_ref)
    pl.semaphore_wait(barrier, inner - 1 + chips - 1 + 1)
    send_states(0)
    make_states(1, q_ref, d_ref)
    send_states(1)
    for kind in range(2):
        sum_within(kind)
        send_pair(kind)
        sum_across(kind)
        send_sums(kind)

    for kind in range(2):

        @pl.loop(1, inner)
        def _(step):
            source = (me + inner - step) % inner
            out_copy(kind, source, source).wait_recv()

    for kind in range(2):

        @pl.loop(1, inner)
        def _(step):
            peer = (me + step) % inner
            in_copy(kind, peer, me).wait_send()
            out_copy(kind, peer, me).wait_send()

        @pl.loop(1, chips)
        def _(step):
            z_copy(kind, (z + step) % chips, z).wait_send()

        total_copy(kind).wait_send()
        carried_copy(kind, my_rows).wait_send()


def outputs_kernel(scale, q_ref, k_ref, v_ref, d_ref, s_ref, o_ref, gq_ref, gk_ref, gv_ref):
    rows = q_ref.shape[0]
    lower = lax.broadcasted_iota(jnp.int32, (rows, rows), 0) >= lax.broadcasted_iota(
        jnp.int32, (rows, rows), 1
    )
    for h in range(q_ref.shape[1] // HEAD):
        cols = slice(h * HEAD, (h + 1) * HEAD)
        q, k, v, d = q_ref[:, cols], k_ref[:, cols], v_ref[:, cols], d_ref[:, cols]
        s, g = s_ref[0, h], s_ref[1, h]
        a = jnp.where(lower, dot(q, k, 1, 1), 0.0).astype(jnp.bfloat16)
        b = jnp.where(lower, dot(d, v, 1, 1), 0.0).astype(jnp.bfloat16)
        o_ref[:, cols] = (scale * (dot(q, s, 1, 0) + dot(a, v, 1, 0))).astype(o_ref.dtype)
        gq_ref[:, cols] = (scale * (dot(d, s, 1, 1) + dot(b, k, 1, 0))).astype(gq_ref.dtype)
        gk_ref[:, cols] = (scale * (dot(v, g, 1, 1) + dot(b, q, 0, 0))).astype(gk_ref.dtype)
        gv_ref[:, cols] = (scale * (dot(k, g, 1, 0) + dot(a, d, 0, 0))).astype(gv_ref.dtype)


def body(queries, keys, values, cotangent):
    rows, width = queries.shape
    heads = width // HEAD
    inner, outer = lax.axis_size("inner"), lax.axis_size("outer")
    scale = float(HEAD * rows * inner * outer) ** (-0.5)
    assert inner == 2 * heads
    chips, half, quarter = outer // 2, HEAD // 2, HEAD // 4
    vmem = pl.BlockSpec(memory_space=pltpu.VMEM)
    dma = pltpu.SemaphoreType.DMA

    state = pl.pallas_call(
        functools.partial(exchange_kernel, heads, inner, outer),
        out_shape=jax.ShapeDtypeStruct((2, heads, HEAD, HEAD), jnp.bfloat16),
        in_specs=[vmem] * 4,
        out_specs=vmem,
        scratch_shapes=[
            pltpu.VMEM((2, inner, half, HEAD), jnp.bfloat16),
            pltpu.VMEM((2, inner, half, HEAD), jnp.bfloat16),
            pltpu.VMEM((2, inner, half, HEAD), jnp.float32),
            pltpu.VMEM((2, inner, half, HEAD), jnp.bfloat16),
            pltpu.VMEM((2, half, HEAD), jnp.float32),
            pltpu.VMEM((2, half, HEAD), jnp.float32),
            pltpu.VMEM((2, quarter, HEAD), jnp.bfloat16),
            pltpu.VMEM((2, chips, quarter, HEAD), jnp.bfloat16),
            pltpu.VMEM((2, half, HEAD), jnp.float32),
            dma((2, inner)), dma((2, inner)), dma((2, chips)), dma((2, chips)),
            dma((2, inner)), dma((2, inner)), dma((2, 2)), dma((2, 2)),
        ],
        compiler_params=pltpu.CompilerParams(collective_id=0, has_side_effects=True),
    )(queries, keys, values, cotangent)

    steps = 4
    tokens = pl.BlockSpec((rows, width // steps), lambda i: (0, i))
    return pl.pallas_call(
        functools.partial(outputs_kernel, scale),
        grid=(steps,),
        out_shape=(jax.ShapeDtypeStruct((rows, width), jnp.bfloat16),) * 4,
        in_specs=[tokens] * 4
        + [pl.BlockSpec((2, heads // steps, HEAD, HEAD), lambda i: (0, i, 0, 0))],
        out_specs=(tokens,) * 4,
    )(queries, keys, values, cotangent, state)


def solution(mesh):
    spec = P(("outer", "inner"), None)
    return jax.shard_map(
        body, mesh=mesh, in_specs=(spec,) * 4, out_specs=(spec,) * 4, check_vma=False
    )
```

time: 147 us -> 77.4 us (0.53); the launches traced: 145 us -> 77 us
  blocking collectives: 73.2 us -> 0 us
  Pallas kernels: 10.2 us -> 76.4 us
  waiting for transfers between devices: 43 us -> 0 us
  between operations: 14.1 us -> 0.64 us
  other arithmetic: 3.38 us -> 0 us
    all_to_all x2 -> x0, blocking collectives: 73.2 us -> none  [the longest x1 36.6 us: body(): lax.all_to_all(states, 'inner', split_axis=0, concat_axis=0, tiled=True)]
    pallas_call x2, Pallas kernels: 10.2 us -> 76.4 us  [the longest x1 69.7 us: body(): pl.pallas_call(functools.partial(exchange_kernel, heads, inner, outer), o...]
    all_gather x1 -> x0, waiting for transfers between devices: 43 us -> none  [body(): everything = lax.all_gather(total, 'outer')]
    reduce_sum x2 -> x0, other arithmetic: 2.15 us -> none  [the longest x1 1.37 us: body(): jnp.sum(jnp.where(reached[:, None, None, None], everything, 0.0), 0)]
  transfers between devices with their start and end apart: 1 -> 0, of which waited for: 1 -> 0; matrix products, arithmetic and copies ran while one was open for 1% -> 0% of each run, Pallas kernels for 0% -> 0%
where the time goes in v3:
time: 77.4 us; the launch traced here: 77 us
  Pallas kernels  76.4 us (99%)
    pallas_call x1, Pallas kernels, body(): pl.pallas_call(functools.partial(exchange_kernel, heads, inner, outer), o...  69.7 us
    pallas_call x1, Pallas kernels, body(): pl.pallas_call(functools.partial(outputs_kernel, scale), grid=(steps,), o...  6.71 us

profile of v3, /device:TPU:6, one launch (start us, length us, event | category | flops | bytes accessed | tf_op | source)
XLA Modules:
  0.0 77.0 jit_solution(16934420034122123655)
XLA Ops:
  0.6 69.7 %shard_map.75.s_ref = bf16[2,16,128,128]{3,2,1,0:T(8,128)(2,1)} custom-call(bf16[128,2048]{1,0:T(8,128)(2,1)} %q_ref.3, bf16[128,2048]{1,0:T(8,128)(2,1)} %k_ref.3, bf16[128,2048]{1,0:T(8,128)(2,1)} %v_ref.3, bf16[128,2048]{1,0:T(8,128)(2,1)} %d_ref.3), custom_call_target="tpu_custom_call" | custom-call | tf_op jit(solution)/shard_map/pallas_call | solution.py:206
  70.3 6.7 %shard_map.76 = (bf16[128,2048]{1,0:T(8,128)(2,1)}, bf16[128,2048]{1,0:T(8,128)(2,1)}, bf16[128,2048]{1,0:T(8,128)(2,1)}, bf16[128,2048]{1,0:T(8,128)(2,1)}) custom-call(bf16[128,2048]{1,0:T(8,128)(2,1)} %q_ref.3, bf16[128,2048]{1,0:T(8,128)(2,1)} %k_ref.3, bf16[128,2048]{1,0:T(8,128)(2,1)} %v_ref.3, bf16[128,2048]{1,0:T(8,128)(2,1)} %d_ref.3, ...), custom_call_target="tpu_custom_call" | custom-call | tf_op jit(solution)/shard_map/pallas_call | solution.py:229

commit v4 on v3

--- a/solution.py
+++ b/solution.py
@@ -8,6 +8,7 @@
 from jax.sharding import PartitionSpec as P
 
 HEAD = 128
+LINE = 8
 MESH = pl.DeviceIdType.MESH
 
 
@@ -17,21 +18,34 @@
     )
 
 
+def roles(kind, group, y):
+    w = y if kind == 0 else LINE - 1 - y
+    first = (w + group) % 2 == 0
+    leads = jnp.logical_or(first, w == 0)
+    has_partner = jnp.logical_and(first, w < LINE - 1)
+    follows = jnp.logical_and(jnp.logical_not(first), w > 0)
+    return leads, has_partner, follows
+
+
 def exchange_kernel(
     heads, inner, outer, q_ref, k_ref, v_ref, d_ref, state_ref,
-    states, arrived, prefix, outgoing, total, mate, pair, pairs, carried,
+    states, near, joined, arrived, prefix, outgoing, onward, running, total, mate, pair, pairs, carried,
     in_send, in_recv, z_send, z_recv, out_send, out_recv, core_send, core_recv,
+    near_send, near_recv, on_send, on_recv,
 ):
     me, place = lax.axis_index("inner"), lax.axis_index("outer")
     chips, half, quarter = outer // 2, HEAD // 2, HEAD // 4
     z, core = place // 2, place % 2
+    y = me % LINE
+    some = heads // 2
+    my_group = me % heads // some
     other = (place + 1 - 2 * core, me)
     my_rows = pl.ds(pl.multiple_of(core * quarter, quarter), quarter)
     other_rows = pl.ds(pl.multiple_of((1 - core) * quarter, quarter), quarter)
 
     def in_copy(kind, peer, source):
         return pltpu.make_async_remote_copy(
-            states.at[kind, peer], arrived.at[kind, source],
+            joined.at[kind, peer], arrived.at[kind, source],
             in_send.at[kind, peer], in_recv.at[kind, source],
             device_id=(place, peer), device_id_type=MESH,
         )
@@ -73,28 +87,96 @@
             states[kind, h] = both[:half]
             states[kind, heads + h] = both[half:]
 
-    def send_states(kind):
-        @pl.loop(1, inner)
-        def _(step):
-            in_copy(kind, (me + step) % inner, me).start()
-
-        arrived[kind, me] = states[kind, me]
+    def near_copy(kind, group, part):
+        return pltpu.make_async_remote_copy(
+            states.at[kind, pl.ds(part * heads + group * some, some)], near.at[kind, part],
+            near_send.at[kind, part], near_recv.at[kind, part],
+            device_id=(place, (me + (inner - 1 if kind == 0 else 1)) % inner),
+            device_id_type=MESH,
+        )
+
+    def on_copy(kind, group, i):
+        return pltpu.make_async_remote_copy(
+            onward.at[kind, i], state_ref.at[kind, group * some + i],
+            on_send.at[kind, i], on_recv.at[kind, i],
+            device_id=(place, (me + (1 if kind == 0 else inner - 1)) % inner),
+            device_id_type=MESH,
+        )
+
+    def leads_mine(kind, source):
+        return roles(kind, my_group, source % LINE)[0]
+
+    def send_near(kind):
+        for group in range(2):
+            follows = roles(kind, group, y)[2]
+
+            @pl.when(follows)
+            def _():
+                for part in range(2):
+                    near_copy(kind, group, part).start()
+
+    def send_joined(kind):
+        for group in range(2):
+            leads, has_partner, _ = roles(kind, group, y)
+
+            @pl.when(has_partner)
+            def _():
+                for part in range(2):
+                    near_copy(kind, group, part).wait_recv()
+
+            @pl.when(leads)
+            def _():
+                @pl.loop(0, 2 * some)
+                def _(step):
+                    at = (me + step) % (2 * some)
+                    part, i = at // some, at % some
+                    peer = part * heads + group * some + i
+                    mine = states[kind, peer].astype(jnp.float32)
+
+                    @pl.when(has_partner)
+                    def _():
+                        both = mine + near[kind, part, i].astype(jnp.float32)
+                        joined[kind, peer] = both.astype(joined.dtype)
+
+                    @pl.when(jnp.logical_not(has_partner))
+                    def _():
+                        joined[kind, peer] = mine.astype(joined.dtype)
+
+                    @pl.when(peer != me)
+                    def _():
+                        in_copy(kind, peer, me).start()
+
+                    @pl.when(peer == me)
+                    def _():
+                        arrived[kind, me] = joined[kind, me]
 
     def sum_within(kind):
-        def add_arrived(step, acc):
+        total[kind] = jnp.zeros((half, HEAD), jnp.float32)
+
+        @pl.loop(0, inner)
+        def _(step):
             source = (me + inner - step) % inner
-            in_copy(kind, source, source).wait_recv()
-            return acc + arrived[kind, source].astype(jnp.float32)
-
-        total[kind] = lax.fori_loop(1, inner, add_arrived, states[kind, me].astype(jnp.float32))
+
+            @pl.when(leads_mine(kind, source))
+            def _():
+                @pl.when(source != me)
+                def _():
+                    in_copy(kind, source, source).wait_recv()
+
+                total[kind] += arrived[kind, source].astype(jnp.float32)
+
         total_copy(kind).start()
-
-        def turn(step, acc):
+        running[...] = jnp.zeros((half, HEAD), jnp.float32)
+
+        @pl.loop(0, inner)
+        def _(step):
             at = step if kind == 0 else inner - 1 - step
-            prefix[kind, at] = acc
-            return acc + arrived[kind, at].astype(jnp.float32)
-
-        lax.fori_loop(0, inner, turn, jnp.zeros((half, HEAD), jnp.float32))
+
+            @pl.when(leads_mine(kind, at))
+            def _():
+                before = running[...]
+                prefix[kind, at] = before
+                running[...] = before + arrived[kind, at].astype(jnp.float32)
 
     def send_pair(kind):
         total_copy(kind).wait_recv()
@@ -119,13 +201,48 @@
     def send_sums(kind):
         offset = carried[kind] + jnp.where(core + kind == 1, mate[kind], 0.0)
 
-        @pl.loop(1, inner)
+        @pl.loop(0, inner)
         def _(step):
             peer = (me + step) % inner
-            outgoing[kind, peer] = (prefix[kind, peer] + offset).astype(outgoing.dtype)
-            out_copy(kind, peer, me).start()
-
-        state_at(kind, me)[...] = (prefix[kind, me] + offset).astype(outgoing.dtype)
+
+            @pl.when(leads_mine(kind, peer))
+            def _():
+                whole = (prefix[kind, peer] + offset).astype(outgoing.dtype)
+
+                @pl.when(peer != me)
+                def _():
+                    outgoing[kind, peer] = whole
+                    out_copy(kind, peer, me).start()
+
+                @pl.when(peer == me)
+                def _():
+                    state_at(kind, me)[...] = whole
+
+    def send_onward(kind):
+        for group in range(2):
+            leads, has_partner, _ = roles(kind, group, y)
+
+            @pl.when(leads)
+            def _():
+                @pl.loop(0, some)
+                def _(i):
+                    h = group * some + i
+                    for part in range(2):
+                        source = part * heads + h
+
+                        @pl.when(source != me)
+                        def _():
+                            out_copy(kind, source, source).wait_recv()
+
+                    @pl.when(has_partner)
+                    def _():
+                        for part in range(2):
+                            rows = slice(part * half, (part + 1) * half)
+                            onward[kind, i, rows] = (
+                                state_ref[kind, h, rows].astype(jnp.float32)
+                                + states[kind, part * heads + h].astype(jnp.float32)
+                            ).astype(onward.dtype)
+                        on_copy(kind, group, i).start()
 
     barrier = pltpu.get_barrier_semaphore()
 
@@ -144,29 +261,59 @@
     pl.semaphore_signal(barrier, inc=1, device_id=other, device_id_type=MESH)
     make_states(0, k_ref, v_ref)
     pl.semaphore_wait(barrier, inner - 1 + chips - 1 + 1)
-    send_states(0)
+    send_near(0)
     make_states(1, q_ref, d_ref)
-    send_states(1)
+    send_near(1)
+    for kind in range(2):
+        send_joined(kind)
     for kind in range(2):
         sum_within(kind)
         send_pair(kind)
         sum_across(kind)
         send_sums(kind)
-
-    for kind in range(2):
+    for kind in range(2):
+        send_onward(kind)
+    for kind in range(2):
+        for group in range(2):
+
+            @pl.when(roles(kind, group, y)[2])
+            def _():
+                @pl.loop(0, some)
+                def _(i):
+                    on_copy(kind, group, i).wait_recv()
+
+    for kind in range(2):
+        for group in range(2):
+            leads, has_partner, follows = roles(kind, group, y)
+
+            @pl.when(follows)
+            def _():
+                for part in range(2):
+                    near_copy(kind, group, part).wait_send()
+
+            @pl.when(has_partner)
+            def _():
+                @pl.loop(0, some)
+                def _(i):
+                    on_copy(kind, group, i).wait_send()
+
+            @pl.when(leads)
+            def _():
+                @pl.loop(0, 2 * some)
+                def _(at):
+                    peer = at // some * heads + group * some + at % some
+
+                    @pl.when(peer != me)
+                    def _():
+                        in_copy(kind, peer, me).wait_send()
 
         @pl.loop(1, inner)
         def _(step):
-            source = (me + inner - step) % inner
-            out_copy(kind, source, source).wait_recv()
-
-    for kind in range(2):
-
-        @pl.loop(1, inner)
-        def _(step):
             peer = (me + step) % inner
-            in_copy(kind, peer, me).wait_send()
-            out_copy(kind, peer, me).wait_send()
+
+            @pl.when(leads_mine(kind, peer))
+            def _():
+                out_copy(kind, peer, me).wait_send()
 
         @pl.loop(1, chips)
         def _(step):
@@ -199,7 +346,7 @@
     inner, outer = lax.axis_size("inner"), lax.axis_size("outer")
     scale = float(HEAD * rows * inner * outer) ** (-0.5)
     assert inner == 2 * heads
-    chips, half, quarter = outer // 2, HEAD // 2, HEAD // 4
+    chips, half, quarter, some = outer // 2, HEAD // 2, HEAD // 4, heads // 2
     vmem = pl.BlockSpec(memory_space=pltpu.VMEM)
     dma = pltpu.SemaphoreType.DMA
 
@@ -210,9 +357,13 @@
         out_specs=vmem,
         scratch_shapes=[
             pltpu.VMEM((2, inner, half, HEAD), jnp.bfloat16),
+            pltpu.VMEM((2, 2, some, half, HEAD), jnp.bfloat16),
+            pltpu.VMEM((2, inner, half, HEAD), jnp.bfloat16),
             pltpu.VMEM((2, inner, half, HEAD), jnp.bfloat16),
             pltpu.VMEM((2, inner, half, HEAD), jnp.float32),
             pltpu.VMEM((2, inner, half, HEAD), jnp.bfloat16),
+            pltpu.VMEM((2, some, HEAD, HEAD), jnp.bfloat16),
+            pltpu.VMEM((half, HEAD), jnp.float32),
             pltpu.VMEM((2, half, HEAD), jnp.float32),
             pltpu.VMEM((2, half, HEAD), jnp.float32),
             pltpu.VMEM((2, quarter, HEAD), jnp.bfloat16),
@@ -220,6 +371,7 @@
             pltpu.VMEM((2, half, HEAD), jnp.float32),
             dma((2, inner)), dma((2, inner)), dma((2, chips)), dma((2, chips)),
             dma((2, inner)), dma((2, inner)), dma((2, 2)), dma((2, 2)),
+            dma((2, 2)), dma((2, 2)), dma((2, some)), dma((2, some)),
         ],
         compiler_params=pltpu.CompilerParams(collective_id=0, has_side_effects=True),
     )(queries, keys, values, cotangent)

time: 77.4 us -> 84.9 us (1.097)
  Pallas kernels: 76.4 us -> 83.3 us
    pallas_call x1, Pallas kernels: 69.7 us -> 76.6 us  [body(): pl.pallas_call(functools.partial(exchange_kernel, heads, inner, outer), o...]
where the time goes in v4:
time: 84.9 us; the launch traced here: 84 us
  Pallas kernels  83.3 us (98%)
    pallas_call x1, Pallas kernels, body(): pl.pallas_call(functools.partial(exchange_kernel, heads, inner, outer), o...  76.6 us
    pallas_call x1, Pallas kernels, body(): pl.pallas_call(functools.partial(outputs_kernel, scale), grid=(steps,), o...  6.71 us

profile of v4, /device:TPU:6, one launch (start us, length us, event | category | flops | bytes accessed | tf_op | source)
XLA Modules:
  0.0 84.0 jit_solution(14546641498962967300)
XLA Ops:
  0.6 76.6 %shard_map.75.s_ref = bf16[2,16,128,128]{3,2,1,0:T(8,128)(2,1)} custom-call(bf16[128,2048]{1,0:T(8,128)(2,1)} %q_ref.3, bf16[128,2048]{1,0:T(8,128)(2,1)} %k_ref.3, bf16[128,2048]{1,0:T(8,128)(2,1)} %v_ref.3, bf16[128,2048]{1,0:T(8,128)(2,1)} %d_ref.3), custom_call_target="tpu_custom_call" | custom-call | tf_op jit(solution)/shard_map/pallas_call | solution.py:353
  77.3 6.7 %shard_map.76 = (bf16[128,2048]{1,0:T(8,128)(2,1)}, bf16[128,2048]{1,0:T(8,128)(2,1)}, bf16[128,2048]{1,0:T(8,128)(2,1)}, bf16[128,2048]{1,0:T(8,128)(2,1)}) custom-call(bf16[128,2048]{1,0:T(8,128)(2,1)} %q_ref.3, bf16[128,2048]{1,0:T(8,128)(2,1)} %k_ref.3, bf16[128,2048]{1,0:T(8,128)(2,1)} %v_ref.3, bf16[128,2048]{1,0:T(8,128)(2,1)} %d_ref.3, ...), custom_call_target="tpu_custom_call" | custom-call | tf_op jit(solution)/shard_map/pallas_call | solution.py:381

commit v5 on v3

--- a/solution.py
+++ b/solution.py
@@ -32,13 +32,13 @@
     def in_copy(kind, peer, source):
         return pltpu.make_async_remote_copy(
             states.at[kind, peer], arrived.at[kind, source],
-            in_send.at[kind, peer], in_recv.at[kind, source],
+            in_send.at[kind], in_recv.at[kind],
             device_id=(place, peer), device_id_type=MESH,
         )
 
     def z_copy(kind, peer, source):
         return pltpu.make_async_remote_copy(
-            pair.at[kind], pairs.at[kind, source], z_send.at[kind, peer], z_recv.at[kind, source],
+            pair.at[kind], pairs.at[kind, source], z_send.at[kind], z_recv.at[kind],
             device_id=(peer * 2 + core, me), device_id_type=MESH,
         )
 
@@ -49,8 +49,29 @@
     def out_copy(kind, peer, source):
         return pltpu.make_async_remote_copy(
             outgoing.at[kind, peer], state_at(kind, source),
-            out_send.at[kind, peer], out_recv.at[kind, source],
+            out_send.at[kind], out_recv.at[kind],
             device_id=(place, peer), device_id_type=MESH,
+        )
+
+    def all_in(kind):
+        most = pl.ds(0, inner - 1)
+        return pltpu.make_async_remote_copy(
+            states.at[kind, most], arrived.at[kind, most], in_send.at[kind], in_recv.at[kind],
+            device_id=other, device_id_type=MESH,
+        )
+
+    def all_out(kind):
+        most = pl.ds(0, inner - 1)
+        return pltpu.make_async_remote_copy(
+            outgoing.at[kind, most], arrived.at[kind, most], out_send.at[kind], out_recv.at[kind],
+            device_id=other, device_id_type=MESH,
+        )
+
+    def all_z(kind):
+        most = pl.ds(0, chips - 1)
+        return pltpu.make_async_remote_copy(
+            pairs.at[kind, most], pairs.at[kind, most], z_send.at[kind], z_recv.at[kind],
+            device_id=other, device_id_type=MESH,
         )
 
     def total_copy(kind):
@@ -74,72 +95,58 @@
             states[kind, heads + h] = both[half:]
 
     def send_states(kind):
-        @pl.loop(1, inner)
-        def _(step):
-            in_copy(kind, (me + step) % inner, me).start()
+        for step in range(1, inner):
+            in_copy(kind, lax.rem(me + step, inner), me).start()
 
         arrived[kind, me] = states[kind, me]
 
     def sum_within(kind):
-        def add_arrived(step, acc):
-            source = (me + inner - step) % inner
-            in_copy(kind, source, source).wait_recv()
-            return acc + arrived[kind, source].astype(jnp.float32)
-
-        total[kind] = lax.fori_loop(1, inner, add_arrived, states[kind, me].astype(jnp.float32))
-        total_copy(kind).start()
-
-        def turn(step, acc):
+        all_in(kind).wait_recv()
+        acc = jnp.zeros((half, HEAD), jnp.float32)
+        for step in range(inner):
             at = step if kind == 0 else inner - 1 - step
             prefix[kind, at] = acc
-            return acc + arrived[kind, at].astype(jnp.float32)
-
-        lax.fori_loop(0, inner, turn, jnp.zeros((half, HEAD), jnp.float32))
+            acc = acc + arrived[kind, at].astype(jnp.float32)
+        total[kind] = acc
+        total_copy(kind).start()
 
     def send_pair(kind):
         total_copy(kind).wait_recv()
         pair[kind] = (total[kind, my_rows] + mate[kind, my_rows]).astype(pair.dtype)
 
-        @pl.loop(1, chips)
-        def _(step):
-            z_copy(kind, (z + step) % chips, z).start()
+        for step in range(1, chips):
+            z_copy(kind, lax.rem(z + step, chips), z).start()
 
     def sum_across(kind):
-        def add_pair(step, acc):
-            source = (z + chips - step) % chips
-            z_copy(kind, source, source).wait_recv()
+        all_z(kind).wait_recv()
+        acc = jnp.zeros((quarter, HEAD), jnp.float32)
+        for source in range(chips):
             reached = source < z if kind == 0 else source > z
-            return acc + jnp.where(reached, pairs[kind, source].astype(jnp.float32), 0.0)
-
-        zeros = jnp.zeros((quarter, HEAD), jnp.float32)
-        carried[kind, my_rows] = lax.fori_loop(1, chips, add_pair, zeros)
+            acc = acc + jnp.where(reached, pairs[kind, source].astype(jnp.float32), 0.0)
+        carried[kind, my_rows] = acc
         carried_copy(kind, my_rows).start()
         carried_copy(kind, other_rows).wait_recv()
 
     def send_sums(kind):
         offset = carried[kind] + jnp.where(core + kind == 1, mate[kind], 0.0)
 
-        @pl.loop(1, inner)
-        def _(step):
-            peer = (me + step) % inner
+        for peer in range(inner):
             outgoing[kind, peer] = (prefix[kind, peer] + offset).astype(outgoing.dtype)
-            out_copy(kind, peer, me).start()
+
+        for step in range(1, inner):
+            out_copy(kind, lax.rem(me + step, inner), me).start()
 
         state_at(kind, me)[...] = (prefix[kind, me] + offset).astype(outgoing.dtype)
 
     barrier = pltpu.get_barrier_semaphore()
 
-    @pl.loop(1, inner)
-    def _(step):
-        pl.semaphore_signal(
-            barrier, inc=1, device_id=(place, (me + step) % inner), device_id_type=MESH
-        )
-
-    @pl.loop(1, chips)
-    def _(step):
-        pl.semaphore_signal(
-            barrier, inc=1, device_id=((z + step) % chips * 2 + core, me), device_id_type=MESH
-        )
+    for step in range(1, inner):
+        peer = (place, lax.rem(me + step, inner))
+        pl.semaphore_signal(barrier, inc=1, device_id=peer, device_id_type=MESH)
+
+    for step in range(1, chips):
+        peer = (lax.rem(z + step, chips) * 2 + core, me)
+        pl.semaphore_signal(barrier, inc=1, device_id=peer, device_id_type=MESH)
 
     pl.semaphore_signal(barrier, inc=1, device_id=other, device_id_type=MESH)
     make_states(0, k_ref, v_ref)
@@ -154,26 +161,14 @@
         send_sums(kind)
 
     for kind in range(2):
-
-        @pl.loop(1, inner)
-        def _(step):
-            source = (me + inner - step) % inner
-            out_copy(kind, source, source).wait_recv()
-
-    for kind in range(2):
-
-        @pl.loop(1, inner)
-        def _(step):
-            peer = (me + step) % inner
-            in_copy(kind, peer, me).wait_send()
-            out_copy(kind, peer, me).wait_send()
-
-        @pl.loop(1, chips)
-        def _(step):
-            z_copy(kind, (z + step) % chips, z).wait_send()
-
+        all_in(kind).wait_send()
+        all_z(kind).wait_send()
         total_copy(kind).wait_send()
         carried_copy(kind, my_rows).wait_send()
+
+    for kind in range(2):
+        all_out(kind).wait_send()
+        all_out(kind).wait_recv()
 
 
 def outputs_kernel(scale, q_ref, k_ref, v_ref, d_ref, s_ref, o_ref, gq_ref, gk_ref, gv_ref):
@@ -218,8 +213,8 @@
             pltpu.VMEM((2, quarter, HEAD), jnp.bfloat16),
             pltpu.VMEM((2, chips, quarter, HEAD), jnp.bfloat16),
             pltpu.VMEM((2, half, HEAD), jnp.float32),
-            dma((2, inner)), dma((2, inner)), dma((2, chips)), dma((2, chips)),
-            dma((2, inner)), dma((2, inner)), dma((2, 2)), dma((2, 2)),
+            dma((2,)), dma((2,)), dma((2,)), dma((2,)),
+            dma((2,)), dma((2,)), dma((2, 2)), dma((2, 2)),
         ],
         compiler_params=pltpu.CompilerParams(collective_id=0, has_side_effects=True),
     )(queries, keys, values, cotangent)

time: 77.4 us -> 73.7 us (0.952)
  Pallas kernels: 76.4 us -> 72.7 us
    pallas_call x1, Pallas kernels: 69.7 us -> 66 us  [body(): pl.pallas_call(functools.partial(exchange_kernel, heads, inner, outer), o...]
where the time goes in v5:
time: 73.7 us; the launch traced here: 73.4 us
  Pallas kernels  72.7 us (99%)
    pallas_call x1, Pallas kernels, body(): pl.pallas_call(functools.partial(exchange_kernel, heads, inner, outer), o...  66 us
    pallas_call x1, Pallas kernels, body(): pl.pallas_call(functools.partial(outputs_kernel, scale), grid=(steps,), o...  6.71 us

profile of v5, /device:TPU:6, one launch (start us, length us, event | category | flops | bytes accessed | tf_op | source)
XLA Modules:
  0.0 73.4 jit_solution(2060247390552918343)
XLA Ops:
  0.6 66.0 %shard_map.75.s_ref = bf16[2,16,128,128]{3,2,1,0:T(8,128)(2,1)} custom-call(bf16[128,2048]{1,0:T(8,128)(2,1)} %q_ref.3, bf16[128,2048]{1,0:T(8,128)(2,1)} %k_ref.3, bf16[128,2048]{1,0:T(8,128)(2,1)} %v_ref.3, bf16[128,2048]{1,0:T(8,128)(2,1)} %d_ref.3), custom_call_target="tpu_custom_call" | custom-call | tf_op jit(solution)/shard_map/pallas_call | solution.py:201
  66.7 6.7 %shard_map.76 = (bf16[128,2048]{1,0:T(8,128)(2,1)}, bf16[128,2048]{1,0:T(8,128)(2,1)}, bf16[128,2048]{1,0:T(8,128)(2,1)}, bf16[128,2048]{1,0:T(8,128)(2,1)}) custom-call(bf16[128,2048]{1,0:T(8,128)(2,1)} %q_ref.3, bf16[128,2048]{1,0:T(8,128)(2,1)} %k_ref.3, bf16[128,2048]{1,0:T(8,128)(2,1)} %v_ref.3, bf16[128,2048]{1,0:T(8,128)(2,1)} %d_ref.3, ...), custom_call_target="tpu_custom_call" | custom-call | tf_op jit(solution)/shard_map/pallas_call | solution.py:224

commit v6 on v5

--- a/solution.py
+++ b/solution.py
@@ -18,8 +18,9 @@
 
 
 def exchange_kernel(
-    heads, inner, outer, q_ref, k_ref, v_ref, d_ref, state_ref,
-    states, arrived, prefix, outgoing, total, mate, pair, pairs, carried,
+    heads, inner, outer, scale, q_ref, k_ref, v_ref, d_ref,
+    o_out, gq_out, part_k_out, part_v_out, g_ref,
+    s_ref, o_ref, gq_ref, part_k_ref, part_v_ref, put, states, arrived, prefix, outgoing, total, mate, pair, pairs, carried,
     in_send, in_recv, z_send, z_recv, out_send, out_recv, core_send, core_recv,
 ):
     me, place = lax.axis_index("inner"), lax.axis_index("outer")
@@ -44,7 +45,7 @@
 
     def state_at(kind, source):
         rows = pl.ds(pl.multiple_of(source // heads * half, half), half)
-        return state_ref.at[kind, source % heads, rows]
+        return (s_ref, g_ref)[kind].at[source % heads, rows]
 
     def out_copy(kind, peer, source):
         return pltpu.make_async_remote_copy(
@@ -137,6 +138,29 @@
             out_copy(kind, lax.rem(me + step, inner), me).start()
 
         state_at(kind, me)[...] = (prefix[kind, me] + offset).astype(outgoing.dtype)
+
+    def use_sums_before():
+        rows = q_ref.shape[0]
+        lower = lax.broadcasted_iota(jnp.int32, (rows, rows), 0) >= lax.broadcasted_iota(
+            jnp.int32, (rows, rows), 1
+        )
+        for h in range(heads):
+            cols = slice(h * HEAD, (h + 1) * HEAD)
+            q, k, v, d = q_ref[:, cols], k_ref[:, cols], v_ref[:, cols], d_ref[:, cols]
+            s = s_ref[h]
+            a = jnp.where(lower, dot(q, k, 1, 1), 0.0).astype(jnp.bfloat16)
+            b = jnp.where(lower, dot(d, v, 1, 1), 0.0).astype(jnp.bfloat16)
+            o_ref[:, cols] = (scale * (dot(q, s, 1, 0) + dot(a, v, 1, 0))).astype(o_ref.dtype)
+            gq_ref[:, cols] = (scale * (dot(d, s, 1, 1) + dot(b, k, 1, 0))).astype(gq_ref.dtype)
+            part_k_ref[:, cols] = dot(b, q, 0, 0)
+            part_v_ref[:, cols] = dot(a, d, 0, 0)
+
+    puts = [
+        pltpu.make_async_copy(here, there, put.at[i])
+        for i, (here, there) in enumerate(
+            ((o_ref, o_out), (gq_ref, gq_out), (part_k_ref, part_k_out), (part_v_ref, part_v_out))
+        )
+    ]
 
     barrier = pltpu.get_barrier_semaphore()
 
@@ -166,26 +190,27 @@
         total_copy(kind).wait_send()
         carried_copy(kind, my_rows).wait_send()
 
-    for kind in range(2):
-        all_out(kind).wait_send()
-        all_out(kind).wait_recv()
-
-
-def outputs_kernel(scale, q_ref, k_ref, v_ref, d_ref, s_ref, o_ref, gq_ref, gk_ref, gv_ref):
-    rows = q_ref.shape[0]
-    lower = lax.broadcasted_iota(jnp.int32, (rows, rows), 0) >= lax.broadcasted_iota(
-        jnp.int32, (rows, rows), 1
-    )
-    for h in range(q_ref.shape[1] // HEAD):
+    all_out(0).wait_send()
+    all_out(0).wait_recv()
+    use_sums_before()
+    for copy in puts:
+        copy.start()
+    all_out(1).wait_send()
+    for copy in puts:
+        copy.wait()
+    all_out(1).wait_recv()
+
+
+def outputs_kernel(
+    scale, k_ref, v_ref, o_in, gq_in, part_k_ref, part_v_ref, g_ref, o_ref, gq_ref, gk_ref, gv_ref
+):
+    o_ref[...] = o_in[...]
+    gq_ref[...] = gq_in[...]
+    for h in range(k_ref.shape[1] // HEAD):
         cols = slice(h * HEAD, (h + 1) * HEAD)
-        q, k, v, d = q_ref[:, cols], k_ref[:, cols], v_ref[:, cols], d_ref[:, cols]
-        s, g = s_ref[0, h], s_ref[1, h]
-        a = jnp.where(lower, dot(q, k, 1, 1), 0.0).astype(jnp.bfloat16)
-        b = jnp.where(lower, dot(d, v, 1, 1), 0.0).astype(jnp.bfloat16)
-        o_ref[:, cols] = (scale * (dot(q, s, 1, 0) + dot(a, v, 1, 0))).astype(o_ref.dtype)
-        gq_ref[:, cols] = (scale * (dot(d, s, 1, 1) + dot(b, k, 1, 0))).astype(gq_ref.dtype)
-        gk_ref[:, cols] = (scale * (dot(v, g, 1, 1) + dot(b, q, 0, 0))).astype(gk_ref.dtype)
-        gv_ref[:, cols] = (scale * (dot(k, g, 1, 0) + dot(a, d, 0, 0))).astype(gv_ref.dtype)
+        k, v, g = k_ref[:, cols], v_ref[:, cols], g_ref[h]
+        gk_ref[:, cols] = (scale * (dot(v, g, 1, 1) + part_k_ref[:, cols])).astype(gk_ref.dtype)
+        gv_ref[:, cols] = (scale * (dot(k, g, 1, 0) + part_v_ref[:, cols])).astype(gv_ref.dtype)
 
 
 def body(queries, keys, values, cotangent):
@@ -198,12 +223,23 @@
     vmem = pl.BlockSpec(memory_space=pltpu.VMEM)
     dma = pltpu.SemaphoreType.DMA
 
-    state = pl.pallas_call(
-        functools.partial(exchange_kernel, heads, inner, outer),
-        out_shape=jax.ShapeDtypeStruct((2, heads, HEAD, HEAD), jnp.bfloat16),
+    narrow = jax.ShapeDtypeStruct((rows, width), jnp.bfloat16)
+    wide = jax.ShapeDtypeStruct((rows, width), jnp.float32)
+    anywhere = pl.BlockSpec(memory_space=pl.ANY)
+    attended, grad_q, part_k, part_v, later = pl.pallas_call(
+        functools.partial(exchange_kernel, heads, inner, outer, scale),
+        out_shape=(
+            narrow, narrow, wide, wide, jax.ShapeDtypeStruct((heads, HEAD, HEAD), jnp.bfloat16)
+        ),
         in_specs=[vmem] * 4,
-        out_specs=vmem,
+        out_specs=(anywhere,) * 4 + (vmem,),
         scratch_shapes=[
+            pltpu.VMEM((heads, HEAD, HEAD), jnp.bfloat16),
+            pltpu.VMEM((rows, width), jnp.bfloat16),
+            pltpu.VMEM((rows, width), jnp.bfloat16),
+            pltpu.VMEM((rows, width), jnp.float32),
+            pltpu.VMEM((rows, width), jnp.float32),
+            dma((4,)),
             pltpu.VMEM((2, inner, half, HEAD), jnp.bfloat16),
             pltpu.VMEM((2, inner, half, HEAD), jnp.bfloat16),
             pltpu.VMEM((2, inner, half, HEAD), jnp.float32),
@@ -224,11 +260,10 @@
     return pl.pallas_call(
         functools.partial(outputs_kernel, scale),
         grid=(steps,),
-        out_shape=(jax.ShapeDtypeStruct((rows, width), jnp.bfloat16),) * 4,
-        in_specs=[tokens] * 4
-        + [pl.BlockSpec((2, heads // steps, HEAD, HEAD), lambda i: (0, i, 0, 0))],
+        out_shape=(narrow,) * 4,
+        in_specs=[tokens] * 6 + [pl.BlockSpec((heads // steps, HEAD, HEAD), lambda i: (i, 0, 0))],
         out_specs=(tokens,) * 4,
-    )(queries, keys, values, cotangent, state)
+    )(keys, values, attended, grad_q, part_k, part_v, later)
 
 
 def solution(mesh):

time: 73.7 us -> 71.4 us (0.969)
  Pallas kernels: 72.7 us -> 70.4 us
    pallas_call x1, Pallas kernels: 6.71 us -> 4.56 us  [body(): pl.pallas_call(functools.partial(outputs_kernel, scale), grid=(steps,), o...]
where the time goes in v6:
time: 71.4 us; the launch traced here: 71.1 us
  Pallas kernels  70.4 us (99%)
    pallas_call x1, Pallas kernels, body(): pl.pallas_call(functools.partial(exchange_kernel, heads, inner, outer, sc...  65.9 us
    pallas_call x1, Pallas kernels, body(): pl.pallas_call(functools.partial(outputs_kernel, scale), grid=(steps,), o...  4.56 us

profile of v6, /device:TPU:6, one launch (start us, length us, event | category | flops | bytes accessed | tf_op | source)
XLA Modules:
  0.0 71.1 jit_solution(14725437152227943325)
XLA Ops:
  0.6 65.9 %shard_map.75 = (bf16[128,2048]{1,0:T(8,128)(2,1)}, bf16[128,2048]{1,0:T(8,128)(2,1)}, f32[128,2048]{1,0:T(8,128)}, f32[128,2048]{1,0:T(8,128)}, bf16[16,128,128]{2,1,0:T(8,128)(2,1)}) custom-call(bf16[128,2048]{1,0:T(8,128)(2,1)} %q_ref.1, bf16[128,2048]{1,0:T(8,128)(2,1)} %k_ref.3, bf16[128,2048]{1,0:T(8,128)(2,1)} %v_ref.3, bf16[128,2048]{1,0:T(8,128)(2,1)} %d_ref.1), custom_call_target="tpu_custom_call" | custom-call | tf_op jit(solution)/shard_map/pallas_call | solution.py:229
  66.5 4.6 %shard_map.76 = (bf16[128,2048]{1,0:T(8,128)(2,1)}, bf16[128,2048]{1,0:T(8,128)(2,1)}, bf16[128,2048]{1,0:T(8,128)(2,1)}, bf16[128,2048]{1,0:T(8,128)(2,1)}) custom-call(bf16[128,2048]{1,0:T(8,128)(2,1)} %k_ref.3, bf16[128,2048]{1,0:T(8,128)(2,1)} %v_ref.3, bf16[128,2048]{1,0:T(8,128)(2,1)} %get-tuple-element.9.o_in, ...), custom_call_target="tpu_custom_call" | custom-call | tf_op jit(solution)/shard_map/pallas_call | solution.py:260

commit v7 on v6

--- a/solution.py
+++ b/solution.py
@@ -18,8 +18,9 @@
 
 
 def exchange_kernel(
-    heads, inner, outer, scale, q_ref, k_ref, v_ref, d_ref,
+    heads, inner, outer, scale, q_in, k_in, v_in, d_in,
     o_out, gq_out, part_k_out, part_v_out, g_ref,
+    q_ref, k_ref, v_ref, d_ref, get,
     s_ref, o_ref, gq_ref, part_k_ref, part_v_ref, put, states, arrived, prefix, outgoing, total, mate, pair, pairs, carried,
     in_send, in_recv, z_send, z_recv, out_send, out_recv, core_send, core_recv,
 ):
@@ -162,6 +163,15 @@
         )
     ]
 
+    gets = [
+        pltpu.make_async_copy(there, here, get.at[i])
+        for i, (there, here) in enumerate(
+            ((k_in, k_ref), (v_in, v_ref), (q_in, q_ref), (d_in, d_ref))
+        )
+    ]
+    for copy in gets:
+        copy.start()
+
     barrier = pltpu.get_barrier_semaphore()
 
     for step in range(1, inner):
@@ -173,9 +183,13 @@
         pl.semaphore_signal(barrier, inc=1, device_id=peer, device_id_type=MESH)
 
     pl.semaphore_signal(barrier, inc=1, device_id=other, device_id_type=MESH)
+    for copy in gets[:2]:
+        copy.wait()
     make_states(0, k_ref, v_ref)
     pl.semaphore_wait(barrier, inner - 1 + chips - 1 + 1)
     send_states(0)
+    for copy in gets[2:]:
+        copy.wait()
     make_states(1, q_ref, d_ref)
     send_states(1)
     for kind in range(2):
@@ -231,9 +245,11 @@
         out_shape=(
             narrow, narrow, wide, wide, jax.ShapeDtypeStruct((heads, HEAD, HEAD), jnp.bfloat16)
         ),
-        in_specs=[vmem] * 4,
+        in_specs=[anywhere] * 4,
         out_specs=(anywhere,) * 4 + (vmem,),
-        scratch_shapes=[
+        scratch_shapes=[pltpu.VMEM((rows, width), jnp.bfloat16)] * 4
+        + [
+            dma((4,)),
             pltpu.VMEM((heads, HEAD, HEAD), jnp.bfloat16),
             pltpu.VMEM((rows, width), jnp.bfloat16),
             pltpu.VMEM((rows, width), jnp.bfloat16),

time: 71.4 us -> 70.5 us (0.987)
  Pallas kernels: 70.4 us -> 69.1 us
    pallas_call x1, Pallas kernels: 65.9 us -> 64.5 us  [body(): pl.pallas_call(functools.partial(exchange_kernel, heads, inner, outer, sc...]
where the time goes in v7:
time: 70.5 us; the launch traced here: 69.7 us
  Pallas kernels  69.1 us (98%)
    pallas_call x1, Pallas kernels, body(): pl.pallas_call(functools.partial(exchange_kernel, heads, inner, outer, sc...  64.5 us
    pallas_call x1, Pallas kernels, body(): pl.pallas_call(functools.partial(outputs_kernel, scale), grid=(steps,), o...  4.56 us

profile of v7, /device:TPU:6, one launch (start us, length us, event | category | flops | bytes accessed | tf_op | source)
XLA Modules:
  0.0 69.7 jit_solution(5503567340347464919)
XLA Ops:
  0.6 64.5 %shard_map.75 = (bf16[128,2048]{1,0:T(8,128)(2,1)}, bf16[128,2048]{1,0:T(8,128)(2,1)}, f32[128,2048]{1,0:T(8,128)}, f32[128,2048]{1,0:T(8,128)}, bf16[16,128,128]{2,1,0:T(8,128)(2,1)}) custom-call(bf16[128,2048]{1,0:T(8,128)(2,1)} %q_in.1, bf16[128,2048]{1,0:T(8,128)(2,1)} %k_ref.1, bf16[128,2048]{1,0:T(8,128)(2,1)} %v_ref.1, bf16[128,2048]{1,0:T(8,128)(2,1)} %d_in.1), custom_call_target="tpu_custom_call" | custom-call | tf_op jit(solution)/shard_map/pallas_call | solution.py:243
  65.2 4.6 %shard_map.76 = (bf16[128,2048]{1,0:T(8,128)(2,1)}, bf16[128,2048]{1,0:T(8,128)(2,1)}, bf16[128,2048]{1,0:T(8,128)(2,1)}, bf16[128,2048]{1,0:T(8,128)(2,1)}) custom-call(bf16[128,2048]{1,0:T(8,128)(2,1)} %k_ref.1, bf16[128,2048]{1,0:T(8,128)(2,1)} %v_ref.1, bf16[128,2048]{1,0:T(8,128)(2,1)} %get-tuple-element.9.o_in, ...), custom_call_target="tpu_custom_call" | custom-call | tf_op jit(solution)/shard_map/pallas_call | solution.py:276
